TPU v7x, 128 devices: a whole 4x4x4 slice. The times are simulated.
128 devices in a mesh: dp: 16 (over y_hi, x, core), hid: 8 (over y_lo, z).
Axes of the slice: x: 4, y: 4 (y_hi: 2, y_lo: 2; y = y_hi * 2 + y_lo), z: 4, core: 2. Of those that a mesh axis runs over, the one named last changes fastest.
Arguments:
- train_x: bfloat16 [4096, 4096], P('dp', 'hid'), may hold values from -6 to 6
- gate_pre: bfloat16 [4096, 14336], P('dp', 'hid'), may hold values from -6 to 6
- up_pre: bfloat16 [4096, 14336], P('dp', 'hid'), may hold values from -6 to 6
- train_dy: bfloat16 [4096, 4096], P('dp'), may hold values from -6 to 6
- val_x: bfloat16 [512, 4096], P('dp', 'hid'), may hold values from -6 to 6
- val_gate: bfloat16 [512, 14336], P('dp', 'hid'), may hold values from -6 to 6
- val_up: bfloat16 [512, 14336], P('dp', 'hid'), may hold values from -6 to 6
- val_dy: bfloat16 [512, 4096], P('dp'), may hold values from -6 to 6
- down_weight: bfloat16 [14336, 4096], P('hid', 'dp'), may hold values from -0.046875 to 0.046875
Outputs:
- gate_grad: bfloat16 [4096, 14336], P('dp', 'hid')
- up_grad: bfloat16 [4096, 14336], P('dp', 'hid')
- scores: float32 [16, 2], P('dp')
All inputs are finite; a program needn't handle non-finite values.
Results may differ from a plain program's by a relative error of at most 0.0059.
Values may be sent and summed in bfloat16 or wider, within the bound.
A program may use at most 128 MiB of HBM per device.

v0:
```python
import jax
import jax.numpy as jnp
from jax import lax
from jax.sharding import PartitionSpec as P

LEN = 256
step_rate = 0.1


def side_by_side(arrays, axis, dim, along):
    widths = [a.shape[along] for a in arrays]
    both = jnp.concatenate(arrays, axis=along)
    filled = lax.all_gather(both, axis, axis=dim, tiled=True)
    return tuple(jnp.split(filled, [sum(widths[:k]) for k in range(1, len(widths))], axis=along))


def cut_along(shard, dim, peers):
    before, after = (shard.shape[:dim], shard.shape[dim + 1 :])
    return jnp.moveaxis(shard.reshape(*before, peers, -1, *after), dim, 0)


def sum_at_owner(shard, axis, dim):
    parts = cut_along(shard, dim, lax.axis_size(axis))
    arrived = lax.all_to_all(parts, axis, split_axis=0, concat_axis=0, tiled=True)
    return arrived.sum(axis=0)


def sent_to_all(shard, axis):
    copies = jnp.broadcast_to(shard, (lax.axis_size(axis), *shard.shape))
    return lax.all_to_all(copies, axis, split_axis=0, concat_axis=0, tiled=True)


def over_copies(shard, axis):
    return sent_to_all(shard, axis).sum(axis=0)


def backward_parts(hidden_cot, gate, up):
    a = gate.astype(jnp.float32)
    b = up.astype(jnp.float32)
    s = jax.nn.sigmoid(a)
    silu = a * s
    hidden = (silu * b).astype(jnp.bfloat16)
    gate_grad = (hidden_cot * b * s * (1.0 + a * (1.0 - s))).astype(jnp.bfloat16)
    up_grad = (hidden_cot * silu).astype(jnp.bfloat16)
    return (hidden, gate_grad, up_grad)


def pair_dot(left, right):
    return lax.dot_general(
        left, right, (((1,), (1,)), ((), ())), preferred_element_type=jnp.float32
    )


def per_device(train_x, gate_pre, up_pre, train_dy, val_x, val_gate, val_up, val_dy, down_weight):
    n_dp = lax.axis_size("dp")
    n_hid = lax.axis_size("hid")
    dp_me = lax.axis_index("dp")
    hid_me = lax.axis_index("hid")
    tok_rows = train_dy.shape[0]
    val_rows = val_dy.shape[0]
    width = train_x.shape[1]
    n_seq = tok_rows // LEN
    n_val = val_rows * n_dp // LEN
    piece = lax.all_gather(down_weight, "dp", axis=1, tiled=True)
    cot_train = pair_dot(train_dy, piece)
    cot_val = pair_dot(val_dy, piece)
    hidden, gate_grad, up_grad = backward_parts(cot_train, gate_pre, up_pre)
    val_hidden, val_gate_grad, val_up_grad = backward_parts(cot_val, val_gate, val_up)
    offset = hid_me * width
    train_feats = (
        train_x,
        jnp.concatenate([gate_grad, up_grad], axis=1),
        hidden,
        lax.dynamic_slice_in_dim(train_dy, offset, width, 1),
    )
    val_feats = (
        val_x,
        jnp.concatenate([val_gate_grad, val_up_grad], axis=1),
        val_hidden,
        lax.dynamic_slice_in_dim(val_dy, offset, width, 1),
    )
    share = tok_rows // n_hid
    row_seq = (hid_me * share + jnp.arange(share, dtype=jnp.int32)) // LEN
    seq_onehot = (row_seq[:, None] == jnp.arange(n_seq, dtype=jnp.int32)[None, :]).astype(
        jnp.float32
    )

    def grams(block):
        return jnp.stack([pair_dot(block[k], train_feats[k]) for k in range(4)])

    def absorb(state, block, source):
        return lax.dynamic_update_slice(state, grams(block), (0, source * val_rows, 0))

    state = jnp.zeros((4, n_dp * val_rows, tok_rows), jnp.float32)
    state = absorb(state, val_feats, dp_me)
    gathered = side_by_side((val_feats[0], val_feats[1], val_feats[2], val_feats[3]), "dp", 0, 1)

    def visit(step, current):
        source = (dp_me + step) % n_dp
        block = tuple(
            (lax.dynamic_slice_in_dim(whole, source * val_rows, val_rows, 0) for whole in gathered)
        )
        return absorb(current, block, source)

    state = lax.fori_loop(1, n_dp, visit, state)
    summed = sum_at_owner(state, "hid", 2)
    pair = summed[0] * summed[1] + summed[2] * summed[3]
    val_seq = jnp.arange(n_dp * val_rows, dtype=jnp.int32) // LEN
    val_onehot = (val_seq[:, None] == jnp.arange(n_val, dtype=jnp.int32)[None, :]).astype(
        jnp.float32
    )
    col_sums = jnp.dot(val_onehot.T, pair, precision=lax.Precision.HIGHEST)
    partial_scores = jnp.dot(col_sums, seq_onehot, precision=lax.Precision.HIGHEST).T
    scores = over_copies(partial_scores, "hid") * (-step_rate / (LEN * LEN))
    return (gate_grad, up_grad, scores)


def solution(mesh):
    return jax.shard_map(
        per_device,
        mesh=mesh,
        in_specs=(
            P("dp", "hid"),
            P("dp", "hid"),
            P("dp", "hid"),
            P("dp", None),
            P("dp", "hid"),
            P("dp", "hid"),
            P("dp", "hid"),
            P("dp", None),
            P("hid", "dp"),
        ),
        out_specs=(P("dp", "hid"), P("dp", "hid"), P("dp", None)),
        check_vma=False,
    )
```

profile of v0, /device:TPU:0, one launch (start us, length us, event | category | flops | bytes accessed | tf_op | source)
XLA Modules:
  0.0 357.7 jit_solution(11475155400102362533)
XLA Ops:
  8.7 115.3 %all-gather.3.cloned.1.call-done = bf16[1792,4096]{1,0:T(8,128)(2,1)} async-done(((bf16[1792,256]{1,0:T(8,128)(2,1)}), bf16[1792,4096]{1,0:T(8,128)(2,1)}) %all-gather.3.cloned.1.call-update) | async-done | bytes 14680080 | tf_op jit(solution)/shard_map/all_gather | solution.py:64
  124.1 10.3 %constant_dynamic-update-slice_fusion.2 = (bf16[32,6400]{1,0:T(8,128)(2,1)S(1)}, bf16[32,1792]{1,0:T(8,128)(2,1)}, f32[32,1792]{1,0:T(8,128)S(1)}) fusion(bf16[32,6400]{1,0:T(8,128)(2,1)S(1)} %constant_dynamic-update-slice_fusion.3, bf16[32,1792]{1,0:T(8,128)(2,1)} %param.16, bf16[32,1792]{1,0:T(8,128)(2,1)} %param.17, bf16[32,4096]{1,0:T(8,128)(2,1)} %param.18, ...), kind=kOutput, calls=%fused_computation.65 | convolution fusion | flops 470450176 | bytes 15630336 | tf_op jit(solution)/shard_map/dot_general | solution.py:49
  139.2 16.7 %multiply_convert_fusion = (bf16[256,1792]{1,0:T(8,128)(2,1)}, bf16[256,1792]{1,0:T(8,128)(2,1)}, bf16[256,1792]{1,0:T(8,128)(2,1)S(1)}) fusion(bf16[256,1792]{1,0:T(8,128)(2,1)} %param.12, bf16[256,1792]{1,0:T(8,128)(2,1)} %param.13, bf16[256,4096]{1,0:T(8,128)(2,1)S(1)} %copy-done, bf16[1792,4096]{1,0:T(8,128)(2,1)} %all-gather.3.cloned.1.call-done), kind=kOutput, calls=%fused_computation.27 | convolution fusion | flops 3765895168 | bytes 21364736 | tf_op jit(solution)/shard_map/dot_general | solution.py:49
  162.2 37.7 %all-gather.5.cloned.1.call-done = bf16[512,6400]{1,0:T(8,128)(2,1)} async-done(((bf16[32,6400]{1,0:T(8,128)(2,1)}), bf16[512,6400]{1,0:T(8,128)(2,1)}) %all-gather.5.cloned.1.call-update) | async-done | bytes 6553616 | tf_op jit(solution)/shard_map/all_gather | solution.py:13
  202.2 4.1 %split.17 = bf16[512,3584]{1,0:T(8,128)(2,1)} slice(bf16[512,6400]{1,0:T(8,128)(2,1)} %all-gather.5.cloned.1.call-done), slice={[0:512], [512:4096]} | slice | bytes 7340032 | tf_op jit(solution)/shard_map/split | solution.py:14
  206.3 2.9 split.18
  209.2 92.0 %while.15 = (s32[]{:T(128)}, f32[4,512,256]{2,1,0:T(8,128)}, s32[]{:T(128)}, bf16[512,512]{1,0:T(8,128)(2,1)}, bf16[256,512]{1,0:T(8,128)(2,1)S(1)}, /*index=5*/...) while((s32[]{:T(128)}, f32[4,512,256]{2,1,0:T(8,128)}, ...), condition=%wide.region_1.2_spmd, body=%wide.region_0.1_spmd.sunk | while | flops 104955920 | bytes 4079960 | solution.py:105
  211.4 2.3 convolution_bitcast_fusion.15
  217.6 2.3 convolution_bitcast_fusion.15
  223.7 2.3 convolution_bitcast_fusion.15
  229.9 2.3 convolution_bitcast_fusion.15
  236.0 2.3 convolution_bitcast_fusion.15
  242.1 2.3 convolution_bitcast_fusion.15
  254.4 2.3 convolution_bitcast_fusion.15
  260.5 2.3 convolution_bitcast_fusion.15
  272.8 2.3 convolution_bitcast_fusion.15
  278.9 2.3 convolution_bitcast_fusion.15
  285.0 2.3 convolution_bitcast_fusion.15
  297.3 2.3 convolution_bitcast_fusion.15
  301.2 2.9 copy.19
  304.1 3.2 copy.20
  307.3 4.5 %all-to-all-start = ((f32[8,4,512,32]{2,3,1,0:T(8,128)}), f32[8,4,512,32]{2,3,1,0:T(8,128)}, u32[]{:S(2)}, u32[]{:S(2)}) async-start(f32[8,4,512,32]{2,3,1,0:T(8,128)} %copy.20), calls=%async_computation | async-start | bytes 4194304 | tf_op jit(solution)/shard_map/all_to_all | solution.py:24
  311.8 26.6 %all-to-all-done = f32[8,4,512,32]{2,3,1,0:T(8,128)} async-done(((f32[8,4,512,32]{2,3,1,0:T(8,128)}), f32[8,4,512,32]{2,3,1,0:T(8,128)}, u32[]{:S(2)}, u32[]{:S(2)}) %all-to-all-start) | async-done | bytes 2097184 | tf_op jit(solution)/shard_map/all_to_all | solution.py:24
  340.7 9.6 %all_to_all.10 = f32[8,1,2]{2,1,0:T(1,128)S(1)} all-to-all(f32[8,1,2]{2,1,0:T(1,128)S(1)} %broadcast_in_dim.10), channel_id=1, replica_groups=mesh['dp'=16,'hid'=8] {'hid'}, dimensions={0} | all-to-all | bytes 128 | tf_op jit(solution)/shard_map/all_to_all | solution.py:30
  (111 shorter events, 82.2 us)
Async XLA Ops:
  7.2 129.6 %copy-start = (bf16[256,4096]{1,0:T(8,128)(2,1)S(1)}, bf16[256,4096]{1,0:T(8,128)(2,1)}, u32[]{:S(2)}) copy-start(bf16[256,4096]{1,0:T(8,128)(2,1)} %param.14) | copy-start | bytes 6291460
  7.2 116.9 %all-gather.3.cloned.1.call-start = ((), (), s32[]{:S(2)}) async-start(), calls=%async_computation.2 | async-start | bytes 15597568 | tf_op jit(solution)/shard_map/all_gather | solution.py:64
  7.9 192.1 %all-gather.5.cloned.1.call-start = ((), (), s32[]{:S(2)}) async-start(), calls=%async_computation.3 | async-start | bytes 6963200 | tf_op jit(solution)/shard_map/all_gather | solution.py:13
  8.7 125.7 %copy-start.2 = (bf16[32,1792]{1,0:T(8,128)(2,1)S(1)}, bf16[32,1792]{1,0:T(8,128)(2,1)}, u32[]{:S(2)}) copy-start(bf16[32,1792]{1,0:T(8,128)(2,1)} %param.16) | copy-start | bytes 344068
  8.7 126.4 %copy-start.7 = (bf16[32,1792]{1,0:T(8,128)(2,1)S(1)}, bf16[32,1792]{1,0:T(8,128)(2,1)}, u32[]{:S(2)}) copy-start(bf16[32,1792]{1,0:T(8,128)(2,1)} %param.17) | copy-start | bytes 344068
  134.4 4.0 %copy-start.1 = (bf16[256,512]{1,0:T(8,128)(2,1)S(1)}, bf16[256,512]{1,0:T(8,128)(2,1)}, u32[]{:S(2)}) copy-start(bf16[256,512]{1,0:T(8,128)(2,1)} %param.11) | copy-start | bytes 786436
  134.4 4.0 %copy-start.9 = (bf16[32,512]{1,0:T(8,128)(2,1)S(1)}, bf16[32,512]{1,0:T(8,128)(2,1)}, u32[]{:S(2)}) copy-start(bf16[32,512]{1,0:T(8,128)(2,1)} %param.15) | copy-start | bytes 98308
  136.0 0.8 copy-start.6
  155.9 2.3 copy-start.3
  155.9 2.3 copy-start.8
  158.2 2.0 copy-start.10
  158.2 2.0 copy-start.11
  158.2 2.7 copy-start.4
  158.2 2.6 copy-start.5
  307.3 31.1 %all-to-all-start = ((f32[8,4,512,32]{2,3,1,0:T(8,128)}), f32[8,4,512,32]{2,3,1,0:T(8,128)}, u32[]{:S(2)}, u32[]{:S(2)}) async-start(f32[8,4,512,32]{2,3,1,0:T(8,128)} %copy.20), calls=%async_computation | async-start | bytes 4194304 | tf_op jit(solution)/shard_map/all_to_all | solution.py:24
Sparse Core Ops, SparseCore 0:
  10.3 113.7 all-gather.2
  136.9 63.0 all-gather.4
where the time goes:
time: 361 us; the launch traced here: 358 us
  waiting for transfers between devices  180 us (50%)
  matrix products  114 us (32%)
  local copies, waits for them, and re-layouts  19.3 us (5%)
  other arithmetic  15.4 us (4%)
  between operations  14.2 us (4%)
  blocking collectives  9.56 us (3%)
  starting transfers between devices  4.53 us (1%)
    all_gather x1, waiting for transfers between devices, per_device(): piece = lax.all_gather(down_weight, 'dp', axis=1, tiled=True)  115 us
    dot_general x66, matrix products, pair_dot(): lax.dot_general(left, right, (((1,), (1,)), ((), ())), preferred_element_...  114 us
    all_gather x1, waiting for transfers between devices, side_by_side(): filled = lax.all_gather(both, axis, axis=dim, tiled=True)  37.7 us
    all_to_all x1, waiting for transfers between devices, sum_at_owner(): lax.all_to_all(parts, axis, split_axis=0, concat_axis=0, tiled=True)  26.6 us
    dynamic_update_slice x16, other arithmetic, absorb(): lax.dynamic_update_slice(state, grams(block), (0, source * val_rows, 0))  10.8 us
    all_to_all x1, blocking collectives, sent_to_all(): return lax.all_to_all(copies, axis, split_axis=0, concat_axis=0, tiled=True)  9.56 us
    split x3, local copies, waits for them, and re-layouts, side_by_side(): jnp.split(filled, [sum(widths[:k]) for k in range(1, len(widths))], axis=...  9.24 us
  transfers between devices with their start and end apart: 3, of which 3 were waited for; matrix products, arithmetic and copies ran while one was open for 7% of the time, Pallas kernels for 0%

commit v1 on v0

--- a/solution.py
+++ b/solution.py
@@ -61,7 +61,9 @@
     width = train_x.shape[1]
     n_seq = tok_rows // LEN
     n_val = val_rows * n_dp // LEN
-    piece = lax.all_gather(down_weight, "dp", axis=1, tiled=True)
+    piece = jnp.concatenate(
+        lax.all_to_all(jnp.stack([down_weight] * lax.axis_size("dp")), "dp", 0, 0), axis=1
+    )
     cot_train = pair_dot(train_dy, piece)
     cot_val = pair_dot(val_dy, piece)
     hidden, gate_grad, up_grad = backward_parts(cot_train, gate_pre, up_pre)

time: 361 us -> 457 us (1.27)
  waiting for transfers between devices: 180 us -> 274 us
  matrix products: 114 us -> 102 us
  local copies, waits for them, and re-layouts: 19.3 us -> 26.6 us
  starting transfers between devices: 4.53 us -> 11.8 us
    all_to_all x0 -> x1, waiting for transfers between devices: none -> 197 us  [per_device(): lax.all_to_all(jnp.stack([down_weight] * lax.axis_size('dp')), 'dp', 0, 0)]
    all_gather x1 -> x0, waiting for transfers between devices: 115 us -> none  [per_device(): piece = lax.all_gather(down_weight, 'dp', axis=1, tiled=True)]
    all_gather x1, waiting for transfers between devices: 37.7 us -> 50.9 us  [side_by_side(): filled = lax.all_gather(both, axis, axis=dim, tiled=True)]
    dot_general x66, matrix products: 114 us -> 102 us  [pair_dot(): lax.dot_general(left, right, (((1,), (1,)), ((), ())), preferred_element_...]
    all_to_all x0 -> x1, starting transfers between devices: none -> 7.33 us  [per_device(): lax.all_to_all(jnp.stack([down_weight] * lax.axis_size('dp')), 'dp', 0, 0)]
    another operation x0 -> x1, local copies, waits for them, and re-layouts: none -> 6.58 us  [per_device(): jnp.stack([down_weight] * lax.axis_size('dp'))]
  transfers between devices with their start and end apart: 3 -> 3, of which waited for: 3 -> 3; matrix products, arithmetic and copies ran while one was open for 7% -> 3% of each run, Pallas kernels for 0% -> 0%
where the time goes in v1:
time: 457 us; the launch traced here: 454 us
  waiting for transfers between devices  274 us (60%)
  matrix products  102 us (22%)
  local copies, waits for them, and re-layouts  26.6 us (6%)
  other arithmetic  15.4 us (3%)
  between operations  14.2 us (3%)
  starting transfers between devices  11.8 us (3%)
  blocking collectives  9.57 us (2%)
    all_to_all x1, waiting for transfers between devices, per_device(): lax.all_to_all(jnp.stack([down_weight] * lax.axis_size('dp')), 'dp', 0, 0)  197 us
    dot_general x66, matrix products, pair_dot(): lax.dot_general(left, right, (((1,), (1,)), ((), ())), preferred_element_...  102 us
    all_gather x1, waiting for transfers between devices, side_by_side(): filled = lax.all_gather(both, axis, axis=dim, tiled=True)  50.9 us
    all_to_all x1, waiting for transfers between devices, sum_at_owner(): lax.all_to_all(parts, axis, split_axis=0, concat_axis=0, tiled=True)  26.6 us
    dynamic_update_slice x16, other arithmetic, absorb(): lax.dynamic_update_slice(state, grams(block), (0, source * val_rows, 0))  10.8 us
    all_to_all x1, blocking collectives, sent_to_all(): return lax.all_to_all(copies, axis, split_axis=0, concat_axis=0, tiled=True)  9.57 us
    split x3, local copies, waits for them, and re-layouts, side_by_side(): jnp.split(filled, [sum(widths[:k]) for k in range(1, len(widths))], axis=...  9.24 us
  transfers between devices with their start and end apart: 3, of which 3 were waited for; matrix products, arithmetic and copies ran while one was open for 3% of the time, Pallas kernels for 0%

profile of v1, /device:TPU:0, one launch (start us, length us, event | category | flops | bytes accessed | tf_op | source)
XLA Modules:
  0.0 454.0 jit_solution(4025451079586837540)
XLA Ops:
  8.8 6.6 %stack.84 = bf16[16,1792,256]{1,2,0:T(8,128)(2,1)} broadcast(bf16[1792,256]{0,1:T(8,128)(2,1)S(1)} %copy.22), dimensions={1,2} | broadcast | bytes 15597568 | tf_op jit(solution)/shard_map/stack | solution.py:65
  15.4 7.3 %all-to-all-start = ((bf16[16,1792,256]{1,2,0:T(8,128)(2,1)}), bf16[16,1792,256]{1,2,0:T(8,128)(2,1)}, u32[]{:S(2)}, u32[]{:S(2)}) async-start(bf16[16,1792,256]{1,2,0:T(8,128)(2,1)} %stack.84), calls=%async_computation | async-start | bytes 29360128 | tf_op jit(solution)/shard_map/all_to_all | solution.py:65
  22.8 196.7 %all-to-all-done = bf16[16,1792,256]{1,2,0:T(8,128)(2,1)} async-done(((bf16[16,1792,256]{1,2,0:T(8,128)(2,1)}), bf16[16,1792,256]{1,2,0:T(8,128)(2,1)}, u32[]{:S(2)}, u32[]{:S(2)}) %all-to-all-start) | async-done | bytes 14680096 | tf_op jit(solution)/shard_map/all_to_all | solution.py:65
  219.6 8.4 %constant_dynamic-update-slice_fusion.2 = (bf16[32,6400]{1,0:T(8,128)(2,1)S(1)}, bf16[32,1792]{1,0:T(8,128)(2,1)}, f32[32,1792]{1,0:T(8,128)S(1)}) fusion(bf16[32,6400]{1,0:T(8,128)(2,1)S(1)} %constant_dynamic-update-slice_fusion.3, bf16[32,1792]{1,0:T(8,128)(2,1)S(1)} %copy-done.2, bf16[32,1792]{1,0:T(8,128)(2,1)S(1)} %copy-done.8, ...), kind=kOutput, calls=%fused_computation.65 | convolution fusion | flops 470450176 | bytes 15630336 | tf_op jit(solution)/shard_map/dot_general | solution.py:49
  230.0 10.1 %multiply_convert_fusion = (bf16[256,1792]{1,0:T(8,128)(2,1)S(1)}, bf16[256,1792]{1,0:T(8,128)(2,1)S(1)}, bf16[256,1792]{1,0:T(8,128)(2,1)S(1)}) fusion(bf16[256,1792]{1,0:T(8,128)(2,1)} %param.12, bf16[256,1792]{1,0:T(8,128)(2,1)} %param.13, bf16[256,4096]{1,0:T(8,128)(2,1)S(1)} %copy-done, bf16[1792,4096]{0,1:T(8,128)(2,1)} %bitcast.5), kind=kOutput, calls=%fused_computation.27 | convolution fusion | flops 3765895168 | bytes 21364736 | tf_op jit(solution)/shard_map/dot_general | solution.py:49
  245.4 50.9 %all-gather.2.cloned.1.call-done = bf16[512,6400]{1,0:T(8,128)(2,1)} async-done(((bf16[32,6400]{1,0:T(8,128)(2,1)}), bf16[512,6400]{1,0:T(8,128)(2,1)}) %all-gather.2.cloned.1.call-update) | async-done | bytes 6553616 | tf_op jit(solution)/shard_map/all_gather | solution.py:13
  298.5 4.1 split.17
  302.5 2.9 split.18
  305.5 92.0 %while.15 = (s32[]{:T(128)}, f32[4,512,256]{2,1,0:T(8,128)}, s32[]{:T(128)}, bf16[512,512]{1,0:T(8,128)(2,1)}, bf16[256,512]{1,0:T(8,128)(2,1)S(1)}, /*index=5*/...) while((s32[]{:T(128)}, f32[4,512,256]{2,1,0:T(8,128)}, ...), condition=%wide.region_1.2_spmd, body=%wide.region_0.1_spmd.sunk | while | flops 104955920 | bytes 4079960 | solution.py:107
  307.7 2.3 convolution_bitcast_fusion.15
  320.0 2.3 convolution_bitcast_fusion.15
  326.1 2.3 convolution_bitcast_fusion.15
  332.2 2.3 convolution_bitcast_fusion.15
  338.4 2.3 convolution_bitcast_fusion.15
  344.5 2.3 convolution_bitcast_fusion.15
  350.6 2.3 convolution_bitcast_fusion.15
  356.8 2.3 convolution_bitcast_fusion.15
  362.9 2.3 convolution_bitcast_fusion.15
  393.6 2.3 convolution_bitcast_fusion.15
  397.5 2.9 copy.23
  400.4 3.2 copy.24
  403.6 4.5 all-to-all-start.1
  408.0 26.6 %all-to-all-done.1 = f32[8,4,512,32]{2,3,1,0:T(8,128)} async-done(((f32[8,4,512,32]{2,3,1,0:T(8,128)}), f32[8,4,512,32]{2,3,1,0:T(8,128)}, u32[]{:S(2)}, u32[]{:S(2)}) %all-to-all-start.1) | async-done | bytes 2097184 | tf_op jit(solution)/shard_map/all_to_all | solution.py:24
  437.0 9.6 %all_to_all.15 = f32[8,1,2]{2,1,0:T(1,128)S(1)} all-to-all(f32[8,1,2]{2,1,0:T(1,128)S(1)} %broadcast_in_dim.10), channel_id=1, replica_groups=mesh['dp'=16,'hid'=8] {'hid'}, dimensions={0} | all-to-all | bytes 128 | tf_op jit(solution)/shard_map/all_to_all | solution.py:30
  (114 shorter events, 83.1 us)
Async XLA Ops:
  7.2 222.4 %copy-start = (bf16[256,4096]{1,0:T(8,128)(2,1)S(1)}, bf16[256,4096]{1,0:T(8,128)(2,1)}, u32[]{:S(2)}) copy-start(bf16[256,4096]{1,0:T(8,128)(2,1)} %param.14) | copy-start | bytes 6291460
  15.4 7.4 %copy-start.10 = (bf16[32,512]{1,0:T(8,128)(2,1)S(1)}, bf16[32,512]{1,0:T(8,128)(2,1)}, u32[]{:S(2)}) copy-start(bf16[32,512]{1,0:T(8,128)(2,1)} %param.15) | copy-start | bytes 98308
  15.4 204.2 %copy-start.2 = (bf16[32,1792]{1,0:T(8,128)(2,1)S(1)}, bf16[32,1792]{1,0:T(8,128)(2,1)}, u32[]{:S(2)}) copy-start(bf16[32,1792]{1,0:T(8,128)(2,1)} %param.16) | copy-start | bytes 344068
  15.4 204.2 %copy-start.6 = (bf16[32,4096]{1,0:T(8,128)(2,1)S(1)}, bf16[32,4096]{1,0:T(8,128)(2,1)}, u32[]{:S(2)}) copy-start(bf16[32,4096]{1,0:T(8,128)(2,1)} %param.18) | copy-start | bytes 786436
  15.4 204.2 %copy-start.8 = (bf16[32,1792]{1,0:T(8,128)(2,1)S(1)}, bf16[32,1792]{1,0:T(8,128)(2,1)}, u32[]{:S(2)}) copy-start(bf16[32,1792]{1,0:T(8,128)(2,1)} %param.17) | copy-start | bytes 344068
  15.4 204.2 %all-to-all-start = ((bf16[16,1792,256]{1,2,0:T(8,128)(2,1)}), bf16[16,1792,256]{1,2,0:T(8,128)(2,1)}, u32[]{:S(2)}, u32[]{:S(2)}) async-start(bf16[16,1792,256]{1,2,0:T(8,128)(2,1)} %stack.84), calls=%async_computation | async-start | bytes 29360128 | tf_op jit(solution)/shard_map/all_to_all | solution.py:65
  22.7 273.5 %all-gather.2.cloned.1.call-start = ((), (), s32[]{:S(2)}) async-start(), calls=%async_computation.3 | async-start | bytes 6963200 | tf_op jit(solution)/shard_map/all_gather | solution.py:13
  228.0 1.9 copy-start.1
  228.8 0.8 copy-start.7
  230.0 10.2 %copy-start.11 = (bf16[32,1792]{1,0:T(8,128)(2,1)S(1)}, bf16[32,1792]{1,0:T(8,128)(2,1)}, u32[]{:S(2)}) copy-start(bf16[32,1792]{1,0:T(8,128)(2,1)} %get-tuple-element.292) | copy-start | bytes 344068
  230.0 10.2 %copy-start.12 = (bf16[32,1792]{1,0:T(8,128)(2,1)S(1)}, bf16[32,1792]{1,0:T(8,128)(2,1)}, u32[]{:S(2)}) copy-start(bf16[32,1792]{1,0:T(8,128)(2,1)} %get-tuple-element.294) | copy-start | bytes 344068
  240.1 3.9 copy-start.4
  240.1 3.9 copy-start.5
  240.2 1.0 copy-start.3
  240.2 1.2 copy-start.9
  403.6 31.1 %all-to-all-start.1 = ((f32[8,4,512,32]{2,3,1,0:T(8,128)}), f32[8,4,512,32]{2,3,1,0:T(8,128)}, u32[]{:S(2)}, u32[]{:S(2)}) async-start(f32[8,4,512,32]{2,3,1,0:T(8,128)} %copy.24), calls=%async_computation.1 | async-start | bytes 4194304 | tf_op jit(solution)/shard_map/all_to_all | solution.py:24
Sparse Core Ops, SparseCore 0:
  229.7 66.4 all-gather.1
